TPU v7x, 256 devices: a whole 4x4x8 slice. The times are simulated.
256 devices in a mesh: pair: 16 (over x, y), col: 16 (over z, core).
Axes of the slice: x: 4, y: 4, z: 8, core: 2. Of those that a mesh axis runs over, the one named last changes fastest.
Arguments:
- w_tiles: float32 [80, 128, 8192], P('pair', 'col'), may hold values from -0.15625 to 0.15625
- w_cols: int32 [80, 128], P('pair', 'col'), may hold values from 0 to 19, as said below
- t_tiles: float32 [320, 16, 4096], P('col', 'pair'), may hold values from -6 to 6
- t_cols: int32 [320, 16], P('col', 'pair'), may hold values from 0 to 79, as said below
- z_cols: int32 [16, 80, 5], P('pair'), may hold values from 0 to 4, as said below
Outputs:
- z_tiles: float32 [16, 80, 5, 8192], P('pair', None, None, 'col')
Inputs may be any that keep to these rules, and one draw needn't show every extreme that they name: `w_cols`: the 8 entries of one row tile and one col index are distinct. `t_cols`: the 16 entries of one contraction tile are distinct. `z_cols`: the 5 entries of one group and row tile name each of the group's column tiles once.
All inputs are finite; a program needn't handle non-finite values.
Results may differ from a plain program's by a relative error of at most 0.00007.
Values sent between devices are 32-bit elements; how exact they have to be, the bound alone decides.
A program may use at most 192 MiB of HBM per device.

v0:
```python
import functools

import jax
import jax.numpy as jnp
from jax import lax
from jax.experimental import pallas as pl
from jax.experimental.pallas import tpu as pltpu
from jax.sharding import PartitionSpec as P

MESH = pl.DeviceIdType.MESH

S = 64
LANES = 128
SIDE = 4
PAIRS = 16
NZ = 8
RT = 5
KC = 20
WS = 8
CW = 5
NB = 8
PL = 5
ROWS = 640
HALF = ROWS // 2
CH = 40
KDIM = KC * S
SHARD = KC * 32
COLS = 80
HS = SHARD // 2
QS = HS // 2
STEPS_A = 4
STEPS_B = 3
DEPTH = 4
PARTS = ((0, 2), (2, 4), (4, 5))
F32 = jnp.float32
BF16 = jnp.bfloat16
PLACES = ((0, 1), (2, 3), (4, 9), (5, 6), (7, 8))


def mix(a, b, left):
    straight = jnp.where(left, a, b)
    crossed = pltpu.roll(jnp.where(left, b, a), S, 1)
    return jnp.where(left, straight, crossed), jnp.where(left, crossed, straight)


def split(x):
    high = x.astype(BF16)
    return high, (x - high.astype(F32)).astype(BF16)


def main_kernel(
    t_ref,
    ids_ref,
    w_ref,
    w_cols_ref,
    out_ref,
    shard,
    tiles,
    ids_own,
    ids,
    inv_vec,
    inv,
    w_rows,
    w_wide,
    w_pair,
    halves,
    t_high,
    t_low,
    part,
    swap,
    acc_a,
    acc_b,
    total,
    g_send,
    g_recv,
    own_sem,
    inv_sem,
    i_send,
    i_recv,
    s_send,
    s_recv,
    a_send,
    a_recv,
    b_send,
    b_recv,
    x_send,
    x_recv,
    home_sem,
):
    p = lax.axis_index("pair")
    q = lax.axis_index("col")
    px, py = p // SIDE, lax.rem(p, SIDE)
    z, core = q // 2, lax.rem(q, 2)
    left = lax.broadcasted_iota(jnp.int32, (1, LANES), 1) < S

    def near(axis, sign):
        if axis == 0:
            there = lax.rem(px + sign + SIDE, SIDE) * SIDE + py
        else:
            there = px * SIDE + lax.rem(py + sign + SIDE, SIDE)
        return {"pair": there, "col": q}

    def along_z(step):
        return {"pair": p, "col": lax.rem(z + step + 2 * NZ, NZ) * 2 + core}

    mate = {"pair": p, "col": z * 2 + 1 - core}

    barrier = pltpu.get_barrier_semaphore()
    for d in range(1, PAIRS):
        pl.semaphore_signal(
            barrier, inc=1, device_id={"pair": lax.rem(p + d, PAIRS), "col": q}, device_id_type=MESH
        )
    for who in (mate, along_z(1), along_z(-1)):
        pl.semaphore_signal(barrier, inc=1, device_id=who, device_id_type=MESH)

    ids_own[...] = jnp.zeros_like(ids_own)
    ids_own[0:1, 0:KC] = ids_ref[...]

    for k in range(KC):
        top = t_ref[k * 32 : k * 32 + 16]
        bottom = t_ref[k * 32 + 16 : k * 32 + 32]
        for h, rows in enumerate(mix(top, bottom, left)):
            shard[pl.ds(k * 32 + h, 16, stride=2), :] = rows

    pl.semaphore_wait(barrier, PAIRS + 2)
    own_copy = pltpu.make_async_copy(shard, tiles.at[p], own_sem)
    own_copy.start()

    def slot(half, da, db):
        dx, dy = (da, db) if half == 0 else (db, da)
        return lax.rem(px + dx + SIDE, SIDE) * SIDE + lax.rem(py + dy + SIDE, SIDE)

    def hop(number, half, da, db, first, count, axis, sign):
        place = slot(half, da, db)
        rows = pl.ds(first, count)
        source = shard.at[rows] if (da, db) == (0, 0) else tiles.at[place, rows]
        return pltpu.make_async_remote_copy(
            src_ref=source,
            dst_ref=tiles.at[place, rows],
            send_sem=g_send.at[number],
            recv_sem=g_recv.at[number],
            device_id=near(axis, sign),
            device_id_type=MESH,
        )

    def landing(number, half, da, db, first, count, axis, sign):
        return pltpu.make_async_remote_copy(
            src_ref=tiles.at[slot(half, da, db), pl.ds(first, count)],
            dst_ref=tiles.at[slot(half, da, db), pl.ds(first, count)],
            send_sem=g_send.at[number],
            recv_sem=g_recv.at[number],
            device_id=near(axis, sign),
            device_id_type=MESH,
        )

    sends = []
    numbers = {}

    def go(half, kind, da, sign):
        axis_a, axis_b = (0, 1) if half == 0 else (1, 0)
        base = half * HS
        quarter = base if sign == 1 else base + QS
        if kind == "a0":
            args = (0, 0, base, HS, axis_a)
            seen = (-sign, 0)
        elif kind == "a1":
            args = (-sign, 0, quarter, QS, axis_a)
            seen = (2, 0)
        elif kind == "b0":
            args = (da, 0, base, HS, axis_b)
            seen = (da, -sign)
        else:
            args = (da, -sign, quarter, QS, axis_b)
            seen = (da, 2)
        number = len(numbers)
        numbers[half, kind, da, sign] = (number, half, *seen, *args[2:], sign)
        copy = hop(number, half, *args, sign)
        copy.start()
        sends.append(copy)

    def got(half, kind, da, sign):
        landing(*numbers[half, kind, da, sign]).wait_recv()

    both = (1, -1)
    for sign in both:
        for half in range(2):
            go(half, "a0", 0, sign)
            go(half, "b0", 0, sign)

    def send_ids(d):
        there = lax.rem(p + d, PAIRS)
        return pltpu.make_async_remote_copy(
            src_ref=ids_own,
            dst_ref=ids.at[p],
            send_sem=i_send.at[there],
            recv_sem=i_recv.at[p],
            device_id={"pair": there, "col": q},
            device_id_type=MESH,
        )

    def get_ids(d):
        source = lax.rem(p + d, PAIRS)
        return pltpu.make_async_remote_copy(
            src_ref=ids_own,
            dst_ref=ids.at[source],
            send_sem=i_send.at[source],
            recv_sem=i_recv.at[source],
            device_id={"pair": source, "col": q},
            device_id_type=MESH,
        )

    for d in range(1, PAIRS):
        send_ids(d).start()
    ids[p] = ids_own[...]

    @pl.loop(0, 64)
    def _(m):
        lanes = pl.ds(pl.multiple_of(m * LANES, LANES), LANES)
        for r in range(RT):
            w_rows[r, pl.ds(m, WS, stride=64), :] = w_ref[r, :, lanes]

    def w_dense(w):
        for r in range(RT):
            picks = [jnp.zeros((64, LANES), F32)] * 2
            for n in range(WS):
                rows = w_rows[r, n * 64 : (n + 1) * 64, :]
                for k in range(2):
                    there = jnp.where(w_cols_ref[r, n] == 2 * w + k, 1.0, 0.0)
                    picks[k] = picks[k] + there * rows
            for odd, rows in enumerate(mix(*picks, left)):
                for zz in range(NZ):
                    for c in range(2):
                        to = c * HALF + zz * CH + r * 8 + odd * 4
                        w_wide[w, to : to + 4, :] = rows[zz * 8 + c * 4 : zz * 8 + c * 4 + 4]

    def w_split(w):
        high, low = split(w_wide[w])
        w_pair[0:ROWS, w * LANES : (w + 1) * LANES] = high
        w_pair[ROWS : 2 * ROWS, w * LANES : (w + 1) * LANES] = low

    def halve(half, da, db):
        place = slot(half, da, db)

        @pl.loop(half * KC // 2, (half + 1) * KC // 2)
        def _(k):
            rows = pl.ds(pl.multiple_of(k * 32, 32), 32)
            x = tiles[place, rows, :]
            turned = pltpu.roll(x, S, 1)
            for h, wide in enumerate((jnp.where(left, x, turned), jnp.where(left, turned, x))):
                high, low = split(wide)
                halves[place, 2 * h, rows, :] = high
                halves[place, 2 * h + 1, rows, :] = low

    for sign in both:
        for half in range(2):
            got(half, "a0", 0, sign)
            go(half, "a1", 0, sign)
            go(half, "b0", -sign, 1)
            go(half, "b0", -sign, -1)

    @pl.loop(0, KC // 4)
    def _(w):
        w_dense(w)

    for sign in both:
        for half in range(2):
            got(half, "b0", 0, sign)
            go(half, "b1", 0, sign)
    for half in range(2):
        for sign in both:
            got(half, "a1", 0, sign)
        for sign in both:
            go(half, "b0", 2, sign)

    @pl.loop(KC // 4, KC // 2)
    def _(w):
        w_dense(w)

    halves[PAIRS] = jnp.zeros((4, SHARD, LANES), BF16)
    own_copy.wait()
    for half in range(2):
        halve(half, 0, 0)
        halve(half, -1, 0)
        halve(half, 1, 0)
        halve(half, 0, -1)
        halve(half, 0, 1)
    for da in (-1, 1):
        for sign in both:
            for half in range(2):
                got(half, "b0", da, sign)
                go(half, "b1", da, sign)
    for w in range(KC // 2):
        w_split(w)
    for sign in both:
        for half in range(2):
            got(half, "b0", 2, sign)
            go(half, "b1", 2, sign)

    for d in range(1, PAIRS):
        get_ids(d).wait_recv()
    tile_at = lax.broadcasted_iota(jnp.int32, (COLS, LANES), 0)
    found = jnp.full((COLS, LANES), PAIRS, jnp.int32)
    for n in range(PAIRS):
        found = jnp.where(ids[n, 0:1, :] == tile_at, n, found)
    inv_vec[...] = found
    table = pltpu.make_async_copy(inv_vec, inv, inv_sem)
    table.start()
    table.wait()
    for half in range(2):
        halve(half, 2, 0)
        for da in (-1, 1, 2):
            halve(half, da, -1)
            halve(half, da, 1)
    for da in (0, -1, 1, 2):
        for half in range(2):
            for sign in both:
                got(half, "b1", da, sign)
            halve(half, da, 2)

    def pair_swap(b, n):
        planes = pl.ds(PARTS[n][0], PARTS[n][1] - PARTS[n][0])
        return pltpu.make_async_remote_copy(
            src_ref=part.at[b, planes, pl.ds((1 - core) * HALF, HALF)],
            dst_ref=swap.at[b, planes],
            send_sem=s_send.at[b, n],
            recv_sem=s_recv.at[b, n],
            device_id=mate,
            device_id_type=MESH,
        )

    def way(b):
        return 1 - 2 * lax.rem(b, 2)

    def own_rows(step):
        return pl.ds(core * HALF + lax.rem(z + step + 2 * NZ, NZ) * CH, CH)

    def chain(b, k, length, acc, send, recv, sign):
        source = part.at[b, :, own_rows(length * sign)] if k == 0 else acc.at[b, k - 1]
        return pltpu.make_async_remote_copy(
            src_ref=source,
            dst_ref=acc.at[b, k],
            send_sem=send.at[b, k],
            recv_sem=recv.at[b, k],
            device_id=along_z(sign),
            device_id_type=MESH,
        )

    def chain_a(b, k):
        return chain(b, k, STEPS_A, acc_a, a_send, a_recv, way(b))

    def chain_b(b, k):
        return chain(b, k, STEPS_B, acc_b, b_send, b_recv, -way(b))

    def group_pair(b):
        return lax.rem(b + p // 2, NB)

    def outward(b, odd):
        there = group_pair(b) * 2 + odd
        return there, pltpu.make_async_remote_copy(
            src_ref=total.at[b, pl.ds(2 * odd, 3)],
            dst_ref=out_ref.at[:, pl.ds(p * CH, CH)],
            send_sem=x_send.at[b, odd],
            recv_sem=x_recv.at[p],
            device_id={"pair": there, "col": q},
            device_id_type=MESH,
        )

    def homeward(b, odd):
        return pltpu.make_async_copy(
            total.at[b, pl.ds(2 * odd, 3)], out_ref.at[:, pl.ds(p * CH, CH)], home_sem
        )

    def only(b, act):
        @pl.when(jnp.logical_and(b >= 0, b < NB))
        def _():
            act(b)

    def begin(b):
        for n in range(len(PARTS)):
            pair_swap(b, n).wait_recv()
        part[b, :, pl.ds(core * HALF, HALF), :] += swap[b]
        chain_a(b, 0).start()
        chain_b(b, 0).start()

    def onward(k):
        def act(b):
            sign = way(b)
            chain_a(b, k).wait_recv()
            acc_a[b, k] += part[b, :, own_rows((STEPS_A - 1 - k) * sign), :]
            chain_a(b, k + 1).start()
            chain_b(b, k).wait_recv()
            if k < STEPS_B - 1:
                acc_b[b, k] += part[b, :, own_rows(-(STEPS_B - 1 - k) * sign), :]
                chain_b(b, k + 1).start()

        return act

    def finish(b):
        chain_a(b, 3).wait_recv()
        total[b] = part[b, :, own_rows(0), :] + acc_a[b, 3] + acc_b[b, 2]
        for odd in range(2):
            there, copy = outward(b, odd)

            @pl.when(there != p)
            def _():
                copy.start()

            @pl.when(there == p)
            def _():
                homeward(b, odd).start()

    def expand(b):
        base = group_pair(b) * 2 * CW

        @pl.loop(0, KC)
        def _(k):
            rows = pl.ds(pl.multiple_of(k * 32, 32), 32)
            for i, (one, two) in enumerate(PLACES):
                a = inv[base + one, k]
                c = inv[base + two, k]
                for h in range(2):
                    to = pl.ds(pl.multiple_of(k * S + h * 32, 32), 32)
                    for n, wide in enumerate((t_high, t_low)):
                        wide[to, i * LANES : (i + 1) * LANES] = jnp.where(
                            left, halves[a, 2 * h + n, rows, :], halves[c, 2 * h + n, rows, :]
                        )

    def multiply(n):
        def act(b):
            first, last = PARTS[n]
            cols = slice(first * LANES, last * LANES)
            wide = jnp.dot(w_pair[...], t_high[:, cols], preferred_element_type=F32)
            thin = jnp.dot(w_pair[0:ROWS, :], t_low[:, cols], preferred_element_type=F32)
            sums = wide[0:ROWS] + (wide[ROWS:] + thin)
            for i in range(first, last):
                part[b, i] = sums[:, (i - first) * LANES : (i - first + 1) * LANES]
            pair_swap(b, n).start()

        return act

    @pl.loop(0, NB + DEPTH)
    def _(t):
        only(t - 4, finish)
        only(t - 2, onward(0))
        only(t, expand)
        only(t - 1, begin)
        only(t, multiply(0))
        only(t - 3, onward(2))
        only(t, multiply(1))
        only(t - 2, onward(1))
        only(t, multiply(2))

    for d in range(1, PAIRS):
        source = lax.rem(p + d, PAIRS)
        pltpu.make_async_remote_copy(
            src_ref=total.at[0, pl.ds(0, 3)],
            dst_ref=out_ref.at[:, pl.ds(source * CH, CH)],
            send_sem=x_send.at[0, 0],
            recv_sem=x_recv.at[source],
            device_id={"pair": source, "col": q},
            device_id_type=MESH,
        ).wait_recv()

    @pl.loop(0, NB)
    def _(b):
        for n in range(len(PARTS)):
            pair_swap(b, n).wait_send()
        for k in range(STEPS_A):
            chain_a(b, k).wait_send()
        for k in range(STEPS_B):
            chain_b(b, k).wait_send()
        for odd in range(2):
            there, copy = outward(b, odd)

            @pl.when(there != p)
            def _():
                copy.wait_send()

            @pl.when(there == p)
            def _():
                homeward(b, odd).wait()

    for copy in sends:
        copy.wait_send()
    for d in range(1, PAIRS):
        send_ids(d).wait_send()


def pick_kernel(rows_ref, z_cols_ref, out_ref):
    odd = lax.rem(lax.axis_index("pair"), 2)
    left = lax.broadcasted_iota(jnp.int32, (1, LANES), 1) < S
    planes = (
        jnp.where(odd == 1, 1, 0),
        jnp.where(odd == 1, 2, 1),
        jnp.where(odd == 1, 0, 2),
    )
    count = out_ref.shape[1]
    across = lax.broadcasted_iota(jnp.int32, (count, count), 1)
    diagonal = lax.broadcasted_iota(jnp.int32, (count, count), 0) == across
    wants = []
    for zz in range(CW):
        row = z_cols_ref[zz : zz + 1, :].astype(F32)
        want = jnp.sum(jnp.where(diagonal, row, 0.0), axis=1, keepdims=True)
        wants.append(jnp.broadcast_to(want, (count, LANES)))
    for j in range(4):
        found = []
        for n, plane in enumerate(planes):
            one = rows_ref[plane, pl.ds(j, count, stride=8), :]
            two = rows_ref[plane, pl.ds(4 + j, count, stride=8), :]
            lefts, rights = mix(one, two, left)
            if n < 2:
                found += [lefts, rights]
            else:
                found.append(jnp.where(odd == 1, rights, lefts))
        for zz in range(CW):
            value = found[0]
            for c in range(1, CW):
                value = jnp.where(wants[zz] == c, found[c], value)
            out_ref[zz, :, j * LANES : (j + 1) * LANES] = value


def on_device(w_tiles, w_cols, t_tiles, t_cols, z_cols):
    t = t_tiles.reshape(SHARD, LANES)
    ids = t_cols.reshape(1, KC)
    vmem = pl.BlockSpec(memory_space=pltpu.VMEM)
    dma = pltpu.SemaphoreType.DMA
    rows = pl.pallas_call(
        main_kernel,
        out_shape=jax.ShapeDtypeStruct((3, PAIRS * CH, LANES), F32),
        in_specs=[vmem, vmem, vmem, pl.BlockSpec(memory_space=pltpu.SMEM)],
        out_specs=pl.BlockSpec(memory_space=pl.ANY),
        scratch_shapes=[
            pltpu.VMEM((SHARD, LANES), F32),
            pltpu.VMEM((PAIRS, SHARD, LANES), F32),
            pltpu.VMEM((8, LANES), jnp.int32),
            pltpu.VMEM((PAIRS, 8, LANES), jnp.int32),
            pltpu.VMEM((COLS, LANES), jnp.int32),
            pltpu.SMEM((COLS, LANES), jnp.int32),
            pltpu.VMEM((RT, WS * 64, LANES), F32),
            pltpu.VMEM((KC // 2, ROWS, LANES), F32),
            pltpu.VMEM((2 * ROWS, KDIM), BF16),
            pltpu.VMEM((PAIRS + 1, 4, SHARD, LANES), BF16),
            pltpu.VMEM((KDIM, PL * LANES), BF16),
            pltpu.VMEM((KDIM, PL * LANES), BF16),
            pltpu.VMEM((NB, PL, ROWS, LANES), F32),
            pltpu.VMEM((NB, PL, HALF, LANES), F32),
            pltpu.VMEM((NB, STEPS_A, PL, CH, LANES), F32),
            pltpu.VMEM((NB, STEPS_B, PL, CH, LANES), F32),
            pltpu.VMEM((NB, PL, CH, LANES), F32),
            dma((40,)),
            dma((40,)),
            dma,
            dma,
            dma((PAIRS,)),
            dma((PAIRS,)),
            dma((NB, len(PARTS))),
            dma((NB, len(PARTS))),
            dma((NB, STEPS_A)),
            dma((NB, STEPS_A)),
            dma((NB, STEPS_B)),
            dma((NB, STEPS_B)),
            dma((NB, 2)),
            dma((PAIRS,)),
            dma,
        ],
        compiler_params=pltpu.CompilerParams(
            collective_id=0, has_side_effects=True, vmem_limit_bytes=66 * 1000 * 1000
        ),
        name="cycle",
    )(t, ids, w_tiles, w_cols)
    picked = pl.pallas_call(
        pick_kernel,
        out_shape=jax.ShapeDtypeStruct((CW, PAIRS * RT, 8 * S), F32),
        in_specs=[vmem, vmem],
        out_specs=vmem,
        name="pick",
    )(rows, z_cols[0].T)
    return picked.transpose(1, 0, 2)[None]


def solution(mesh):
    in_specs = (
        P("pair", "col", None),
        P("pair", "col"),
        P("col", "pair", None),
        P("col", "pair"),
        P("pair", None, None),
    )
    out_specs = P("pair", None, None, "col")
    return jax.shard_map(
        on_device, mesh=mesh, in_specs=in_specs, out_specs=out_specs, check_vma=False
    )
```

profile of v0, /device:TPU:8, one launch (start us, length us, event | category | flops | bytes accessed | tf_op | source)
XLA Modules:
  0.0 155.0 jit_solution(15010436950839924518)
XLA Ops:
  0.0 1.3 copy.8
  1.3 151.2 %cycle.1.rows_ref = f32[3,640,128]{2,1,0:T(8,128)} custom-call(f32[640,128]{1,0:T(8,128)} %bitcast.10, s32[1,20]{1,0:T(1,128)} %bitcast.12, f32[5,8,8192]{2,1,0:T(8,128)} %w_ref.1, s32[5,8]{1,0:T(8,128)} %w_cols_ref.1), custom_call_target="tpu_custom_call" | custom-call | tf_op jit(solution)/shard_map/cycle/pallas_call | solution.py:527
  152.4 2.6 %pick.1 = f32[5,80,512]{2,1,0:T(8,128)} custom-call(f32[3,640,128]{2,1,0:T(8,128)} %cycle.1.rows_ref, s32[5,80]{1,0:T(8,128)} %bitcast.11), custom_call_target="tpu_custom_call" | custom-call | tf_op jit(solution)/shard_map/pick/pallas_call | solution.py:571
where the time goes:
time: 155 us
  Pallas kernels  154 us (99%)
    pallas_call x1, Pallas kernels, on_device(): pl.pallas_call(main_kernel, out_shape=jax.ShapeDtypeStruct((3, PAIRS * CH...  151 us

commit v1 on v0

--- a/solution.py
+++ b/solution.py
@@ -30,8 +30,10 @@
 QS = HS // 2
 STEPS_A = 4
 STEPS_B = 3
-DEPTH = 4
-PARTS = ((0, 2), (2, 4), (4, 5))
+DEPTH = 5
+PARTS = ((0, 3), (3, 5))
+LATE = (9, 7, 5, 3)
+DOTS = (((0, 2), (2, 3)), ((3, 5),))
 F32 = jnp.float32
 BF16 = jnp.bfloat16
 PLACES = ((0, 1), (2, 3), (4, 9), (5, 6), (7, 8))
@@ -241,12 +243,11 @@
     def halve(half, da, db):
         place = slot(half, da, db)
 
-        @pl.loop(half * KC // 2, (half + 1) * KC // 2)
-        def _(k):
-            rows = pl.ds(pl.multiple_of(k * 32, 32), 32)
+        @pl.loop(half * 4, half * 4 + 4)
+        def _(n):
+            rows = pl.ds(pl.multiple_of(n * 80, 80), 80)
             x = tiles[place, rows, :]
-            turned = pltpu.roll(x, S, 1)
-            for h, wide in enumerate((jnp.where(left, x, turned), jnp.where(left, turned, x))):
+            for h, wide in enumerate((x, pltpu.roll(x, S, 1))):
                 high, low = split(wide)
                 halves[place, 2 * h, rows, :] = high
                 halves[place, 2 * h + 1, rows, :] = low
@@ -257,6 +258,11 @@
             go(half, "a1", 0, sign)
             go(half, "b0", -sign, 1)
             go(half, "b0", -sign, -1)
+    own_copy.wait()
+    for half in range(2):
+        halve(half, 0, 0)
+        halve(half, -1, 0)
+        halve(half, 1, 0)
 
     @pl.loop(0, KC // 4)
     def _(w):
@@ -271,24 +277,24 @@
             got(half, "a1", 0, sign)
         for sign in both:
             go(half, "b0", 2, sign)
+    for half in range(2):
+        halve(half, 0, -1)
+        halve(half, 0, 1)
+        halve(half, 2, 0)
 
     @pl.loop(KC // 4, KC // 2)
     def _(w):
         w_dense(w)
 
-    halves[PAIRS] = jnp.zeros((4, SHARD, LANES), BF16)
-    own_copy.wait()
-    for half in range(2):
-        halve(half, 0, 0)
-        halve(half, -1, 0)
-        halve(half, 1, 0)
-        halve(half, 0, -1)
-        halve(half, 0, 1)
     for da in (-1, 1):
         for sign in both:
             for half in range(2):
                 got(half, "b0", da, sign)
                 go(half, "b1", da, sign)
+        for sign in both:
+            for half in range(2):
+                halve(half, da, -sign)
+    halves[PAIRS] = jnp.zeros((4, SHARD, LANES), BF16)
     for w in range(KC // 2):
         w_split(w)
     for sign in both:
@@ -306,50 +312,51 @@
     table = pltpu.make_async_copy(inv_vec, inv, inv_sem)
     table.start()
     table.wait()
-    for half in range(2):
-        halve(half, 2, 0)
-        for da in (-1, 1, 2):
-            halve(half, da, -1)
-            halve(half, da, 1)
+    for sign in both:
+        for half in range(2):
+            halve(half, 2, -sign)
     for da in (0, -1, 1, 2):
         for half in range(2):
             for sign in both:
                 got(half, "b1", da, sign)
             halve(half, da, 2)
 
-    def pair_swap(b, n):
-        planes = pl.ds(PARTS[n][0], PARTS[n][1] - PARTS[n][0])
+    def planes_of(h):
+        return pl.ds(PARTS[h][0], PARTS[h][1] - PARTS[h][0])
+
+    def pair_swap(b, h):
         return pltpu.make_async_remote_copy(
-            src_ref=part.at[b, planes, pl.ds((1 - core) * HALF, HALF)],
-            dst_ref=swap.at[b, planes],
-            send_sem=s_send.at[b, n],
-            recv_sem=s_recv.at[b, n],
+            src_ref=part.at[b, planes_of(h), pl.ds((1 - core) * HALF, HALF)],
+            dst_ref=swap.at[b, planes_of(h)],
+            send_sem=s_send.at[b, h],
+            recv_sem=s_recv.at[b, h],
             device_id=mate,
             device_id_type=MESH,
         )
 
-    def way(b):
-        return 1 - 2 * lax.rem(b, 2)
+    def way(b, h):
+        return 1 - 2 * lax.rem(b + h, 2)
 
     def own_rows(step):
         return pl.ds(core * HALF + lax.rem(z + step + 2 * NZ, NZ) * CH, CH)
 
-    def chain(b, k, length, acc, send, recv, sign):
-        source = part.at[b, :, own_rows(length * sign)] if k == 0 else acc.at[b, k - 1]
+    def chain(b, h, k, length, acc, send, recv, sign):
+        planes = planes_of(h)
+        source = part.at[b, planes, own_rows(length * sign)] if k == 0 else acc.at[b, k - 1, planes]
         return pltpu.make_async_remote_copy(
             src_ref=source,
-            dst_ref=acc.at[b, k],
-            send_sem=send.at[b, k],
-            recv_sem=recv.at[b, k],
+            dst_ref=acc.at[b, k, planes],
+            send_sem=send.at[b, h, k],
+            recv_sem=recv.at[b, h, k],
             device_id=along_z(sign),
             device_id_type=MESH,
         )
 
-    def chain_a(b, k):
-        return chain(b, k, STEPS_A, acc_a, a_send, a_recv, way(b))
-
-    def chain_b(b, k):
-        return chain(b, k, STEPS_B, acc_b, b_send, b_recv, -way(b))
+    def chain_a(b, h, k):
+        return chain(b, h, k, STEPS_A, acc_a, a_send, a_recv, way(b, h))
+
+    def chain_b(b, h, k):
+        return chain(b, h, k, STEPS_B, acc_b, b_send, b_recv, -way(b, h))
 
     def group_pair(b):
         return lax.rem(b + p // 2, NB)
@@ -370,85 +377,93 @@
             total.at[b, pl.ds(2 * odd, 3)], out_ref.at[:, pl.ds(p * CH, CH)], home_sem
         )
 
-    def only(b, act):
-        @pl.when(jnp.logical_and(b >= 0, b < NB))
+    def begin(b, h):
+        pair_swap(b, h).wait_recv()
+        part[b, planes_of(h), pl.ds(core * HALF, HALF), :] += swap[b, planes_of(h)]
+        chain_a(b, h, 0).start()
+        chain_b(b, h, 0).start()
+
+    def onward(k):
+        def act(b, h):
+            sign = way(b, h)
+            planes = planes_of(h)
+            chain_a(b, h, k).wait_recv()
+            acc_a[b, k, planes] += part[b, planes, own_rows((STEPS_A - 1 - k) * sign), :]
+            chain_a(b, h, k + 1).start()
+            chain_b(b, h, k).wait_recv()
+            if k < STEPS_B - 1:
+                acc_b[b, k, planes] += part[b, planes, own_rows(-(STEPS_B - 1 - k) * sign), :]
+                chain_b(b, h, k + 1).start()
+
+        return act
+
+    def finish(b, h):
+        planes = planes_of(h)
+        chain_a(b, h, 3).wait_recv()
+        total[b, planes] = part[b, planes, own_rows(0), :] + acc_a[b, 3, planes] + acc_b[b, 2, planes]
+        there, copy = outward(b, h)
+
+        @pl.when(there != p)
         def _():
-            act(b)
-
-    def begin(b):
-        for n in range(len(PARTS)):
-            pair_swap(b, n).wait_recv()
-        part[b, :, pl.ds(core * HALF, HALF), :] += swap[b]
-        chain_a(b, 0).start()
-        chain_b(b, 0).start()
-
-    def onward(k):
-        def act(b):
-            sign = way(b)
-            chain_a(b, k).wait_recv()
-            acc_a[b, k] += part[b, :, own_rows((STEPS_A - 1 - k) * sign), :]
-            chain_a(b, k + 1).start()
-            chain_b(b, k).wait_recv()
-            if k < STEPS_B - 1:
-                acc_b[b, k] += part[b, :, own_rows(-(STEPS_B - 1 - k) * sign), :]
-                chain_b(b, k + 1).start()
-
-        return act
-
-    def finish(b):
-        chain_a(b, 3).wait_recv()
-        total[b] = part[b, :, own_rows(0), :] + acc_a[b, 3] + acc_b[b, 2]
-        for odd in range(2):
-            there, copy = outward(b, odd)
-
-            @pl.when(there != p)
-            def _():
-                copy.start()
-
-            @pl.when(there == p)
-            def _():
-                homeward(b, odd).start()
-
-    def expand(b):
+            copy.start()
+
+        @pl.when(there == p)
+        def _():
+            homeward(b, h).start()
+
+    def expand(b, h):
         base = group_pair(b) * 2 * CW
 
         @pl.loop(0, KC)
         def _(k):
             rows = pl.ds(pl.multiple_of(k * 32, 32), 32)
-            for i, (one, two) in enumerate(PLACES):
+            for i in range(*PARTS[h]):
+                one, two = PLACES[i]
                 a = inv[base + one, k]
                 c = inv[base + two, k]
-                for h in range(2):
-                    to = pl.ds(pl.multiple_of(k * S + h * 32, 32), 32)
+                for g in range(2):
+                    to = pl.ds(pl.multiple_of(k * S + g * 32, 32), 32)
                     for n, wide in enumerate((t_high, t_low)):
                         wide[to, i * LANES : (i + 1) * LANES] = jnp.where(
-                            left, halves[a, 2 * h + n, rows, :], halves[c, 2 * h + n, rows, :]
+                            left,
+                            halves[a, 2 * g + n, rows, :],
+                            halves[c, 2 - 2 * g + n, rows, :],
                         )
 
     def multiply(n):
-        def act(b):
-            first, last = PARTS[n]
+        def act(b, h):
+            first, last = DOTS[h][n]
             cols = slice(first * LANES, last * LANES)
             wide = jnp.dot(w_pair[...], t_high[:, cols], preferred_element_type=F32)
             thin = jnp.dot(w_pair[0:ROWS, :], t_low[:, cols], preferred_element_type=F32)
             sums = wide[0:ROWS] + (wide[ROWS:] + thin)
             for i in range(first, last):
                 part[b, i] = sums[:, (i - first) * LANES : (i - first + 1) * LANES]
-            pair_swap(b, n).start()
+            if n == len(DOTS[h]) - 1:
+                pair_swap(b, h).start()
 
         return act
 
     @pl.loop(0, NB + DEPTH)
     def _(t):
-        only(t - 4, finish)
-        only(t - 2, onward(0))
-        only(t, expand)
-        only(t - 1, begin)
-        only(t, multiply(0))
-        only(t - 3, onward(2))
-        only(t, multiply(1))
-        only(t - 2, onward(1))
-        only(t, multiply(2))
+        for h in range(2):
+
+            def only(late, act):
+                b, part_of = t + (h - late) // 2, (h - late) % 2
+
+                @pl.when(jnp.logical_and(b >= 0, b < NB))
+                def _():
+                    act(b, part_of)
+
+            only(LATE[0], finish)
+            only(LATE[1], onward(2))
+            only(LATE[2], onward(1))
+            only(LATE[3], onward(0))
+            only(0, expand)
+            only(0, multiply(0))
+            only(1, begin)
+            if len(DOTS[h]) > 1:
+                only(0, multiply(1))
 
     for d in range(1, PAIRS):
         source = lax.rem(p + d, PAIRS)
@@ -463,14 +478,13 @@
 
     @pl.loop(0, NB)
     def _(b):
-        for n in range(len(PARTS)):
-            pair_swap(b, n).wait_send()
-        for k in range(STEPS_A):
-            chain_a(b, k).wait_send()
-        for k in range(STEPS_B):
-            chain_b(b, k).wait_send()
-        for odd in range(2):
-            there, copy = outward(b, odd)
+        for h in range(2):
+            pair_swap(b, h).wait_send()
+            for k in range(STEPS_A):
+                chain_a(b, h, k).wait_send()
+            for k in range(STEPS_B):
+                chain_b(b, h, k).wait_send()
+            there, copy = outward(b, h)
 
             @pl.when(there != p)
             def _():
@@ -478,7 +492,7 @@
 
             @pl.when(there == p)
             def _():
-                homeward(b, odd).wait()
+                homeward(b, h).wait()
 
     for copy in sends:
         copy.wait_send()
@@ -499,7 +513,7 @@
     diagonal = lax.broadcasted_iota(jnp.int32, (count, count), 0) == across
     wants = []
     for zz in range(CW):
-        row = z_cols_ref[zz : zz + 1, :].astype(F32)
+        row = z_cols_ref[zz].astype(F32)
         want = jnp.sum(jnp.where(diagonal, row, 0.0), axis=1, keepdims=True)
         wants.append(jnp.broadcast_to(want, (count, LANES)))
     for j in range(4):
@@ -555,10 +569,10 @@
             dma((PAIRS,)),
             dma((NB, len(PARTS))),
             dma((NB, len(PARTS))),
-            dma((NB, STEPS_A)),
-            dma((NB, STEPS_A)),
-            dma((NB, STEPS_B)),
-            dma((NB, STEPS_B)),
+            dma((NB, 2, STEPS_A)),
+            dma((NB, 2, STEPS_A)),
+            dma((NB, 2, STEPS_B)),
+            dma((NB, 2, STEPS_B)),
             dma((NB, 2)),
             dma((PAIRS,)),
             dma,
@@ -574,7 +588,7 @@
         in_specs=[vmem, vmem],
         out_specs=vmem,
         name="pick",
-    )(rows, z_cols[0].T)
+    )(rows, z_cols.transpose(2, 0, 1))
     return picked.transpose(1, 0, 2)[None]
 
 

time: 155 us -> 128 us (0.83)
  Pallas kernels: 154 us -> 128 us
    pallas_call x1, Pallas kernels: 151 us -> 125 us  [on_device(): pl.pallas_call(main_kernel, out_shape=jax.ShapeDtypeStruct((3, PAIRS * CH...]
where the time goes in v1:
time: 128 us
  Pallas kernels  128 us (100%)
    pallas_call x1, Pallas kernels, on_device(): pl.pallas_call(main_kernel, out_shape=jax.ShapeDtypeStruct((3, PAIRS * CH...  125 us
    pallas_call x1, Pallas kernels, on_device(): pl.pallas_call(pick_kernel, out_shape=jax.ShapeDtypeStruct((CW, PAIRS * R...  2.6 us

profile of v1, /device:TPU:8, one launch (start us, length us, event | category | flops | bytes accessed | tf_op | source)
XLA Modules:
  0.0 127.8 jit_solution(7018801942926755857)
XLA Ops:
  0.0 125.2 %cycle.1.rows_ref = f32[3,640,128]{2,1,0:T(8,128)} custom-call(f32[640,128]{1,0:T(8,128)} %bitcast.6, s32[1,20]{1,0:T(1,128)} %bitcast.8, f32[5,8,8192]{2,1,0:T(8,128)} %w_ref.1, s32[5,8]{1,0:T(8,128)} %w_cols_ref.1), custom_call_target="tpu_custom_call" | custom-call | tf_op jit(solution)/shard_map/cycle/pallas_call | solution.py:541
  125.2 2.6 %pick.1 = f32[5,80,512]{2,1,0:T(8,128)} custom-call(f32[3,640,128]{2,1,0:T(8,128)} %cycle.1.rows_ref, s32[5,1,80]{2,1,0:T(1,128)} %bitcast.7), custom_call_target="tpu_custom_call" | custom-call | tf_op jit(solution)/shard_map/pick/pallas_call | solution.py:585

commit v2 on v1

--- a/solution.py
+++ b/solution.py
@@ -18,8 +18,10 @@
 KC = 20
 WS = 8
 CW = 5
-NB = 8
-PL = 5
+NB = 4
+PL = 10
+NH = 5
+WIDE = 2
 ROWS = 640
 HALF = ROWS // 2
 CH = 40
@@ -30,10 +32,9 @@
 QS = HS // 2
 STEPS_A = 4
 STEPS_B = 3
-DEPTH = 5
-PARTS = ((0, 3), (3, 5))
-LATE = (9, 7, 5, 3)
-DOTS = (((0, 2), (2, 3)), ((3, 5),))
+LATE = (16, 12, 8, 4)
+DEPTH = 4
+FIRST = (0, 2, 5, 7)
 F32 = jnp.float32
 BF16 = jnp.bfloat16
 PLACES = ((0, 1), (2, 3), (4, 9), (5, 6), (7, 8))
@@ -243,7 +244,7 @@
     def halve(half, da, db):
         place = slot(half, da, db)
 
-        @pl.loop(half * 4, half * 4 + 4)
+        @pl.loop(half * 4, half * 4 + 4, unroll=4)
         def _(n):
             rows = pl.ds(pl.multiple_of(n * 80, 80), 80)
             x = tiles[place, rows, :]
@@ -322,7 +323,7 @@
             halve(half, da, 2)
 
     def planes_of(h):
-        return pl.ds(PARTS[h][0], PARTS[h][1] - PARTS[h][0])
+        return pl.ds(WIDE * h, WIDE)
 
     def pair_swap(b, h):
         return pltpu.make_async_remote_copy(
@@ -358,23 +359,23 @@
     def chain_b(b, h, k):
         return chain(b, h, k, STEPS_B, acc_b, b_send, b_recv, -way(b, h))
 
-    def group_pair(b):
-        return lax.rem(b + p // 2, NB)
-
-    def outward(b, odd):
-        there = group_pair(b) * 2 + odd
+    def group_pair(b, i):
+        return lax.rem(2 * b + i + 1 + p // 2, PAIRS // 2)
+
+    def outward(b, g):
+        there = group_pair(b, g // 2) * 2 + g % 2
         return there, pltpu.make_async_remote_copy(
-            src_ref=total.at[b, pl.ds(2 * odd, 3)],
+            src_ref=total.at[b, pl.ds(FIRST[g], 3)],
             dst_ref=out_ref.at[:, pl.ds(p * CH, CH)],
-            send_sem=x_send.at[b, odd],
+            send_sem=x_send.at[b, g],
             recv_sem=x_recv.at[p],
             device_id={"pair": there, "col": q},
             device_id_type=MESH,
         )
 
-    def homeward(b, odd):
+    def homeward(b, g):
         return pltpu.make_async_copy(
-            total.at[b, pl.ds(2 * odd, 3)], out_ref.at[:, pl.ds(p * CH, CH)], home_sem
+            total.at[b, pl.ds(FIRST[g], 3)], out_ref.at[:, pl.ds(p * CH, CH)], home_sem
         )
 
     def begin(b, h):
@@ -401,26 +402,28 @@
         planes = planes_of(h)
         chain_a(b, h, 3).wait_recv()
         total[b, planes] = part[b, planes, own_rows(0), :] + acc_a[b, 3, planes] + acc_b[b, 2, planes]
-        there, copy = outward(b, h)
-
-        @pl.when(there != p)
-        def _():
-            copy.start()
-
-        @pl.when(there == p)
-        def _():
-            homeward(b, h).start()
+        if h > 0:
+            there, copy = outward(b, h - 1)
+
+            @pl.when(there != p)
+            def _():
+                copy.start()
+
+            @pl.when(there == p)
+            def _():
+                homeward(b, h - 1).start()
 
     def expand(b, h):
-        base = group_pair(b) * 2 * CW
-
-        @pl.loop(0, KC)
+        base = [group_pair(b, i) * 2 * CW for i in range(2)]
+
+        @pl.loop(0, KC, unroll=5)
         def _(k):
             rows = pl.ds(pl.multiple_of(k * 32, 32), 32)
-            for i in range(*PARTS[h]):
-                one, two = PLACES[i]
-                a = inv[base + one, k]
-                c = inv[base + two, k]
+            for i in range(WIDE):
+                pair, plane = divmod(WIDE * h + i, len(PLACES))
+                one, two = PLACES[plane]
+                a = inv[base[pair] + one, k]
+                c = inv[base[pair] + two, k]
                 for g in range(2):
                     to = pl.ds(pl.multiple_of(k * S + g * 32, 32), 32)
                     for n, wide in enumerate((t_high, t_low)):
@@ -430,26 +433,20 @@
                             halves[c, 2 - 2 * g + n, rows, :],
                         )
 
-    def multiply(n):
-        def act(b, h):
-            first, last = DOTS[h][n]
-            cols = slice(first * LANES, last * LANES)
-            wide = jnp.dot(w_pair[...], t_high[:, cols], preferred_element_type=F32)
-            thin = jnp.dot(w_pair[0:ROWS, :], t_low[:, cols], preferred_element_type=F32)
-            sums = wide[0:ROWS] + (wide[ROWS:] + thin)
-            for i in range(first, last):
-                part[b, i] = sums[:, (i - first) * LANES : (i - first + 1) * LANES]
-            if n == len(DOTS[h]) - 1:
-                pair_swap(b, h).start()
-
-        return act
+    def multiply(b, h):
+        wide = jnp.dot(w_pair[...], t_high[...], preferred_element_type=F32)
+        thin = jnp.dot(w_pair[0:ROWS, :], t_low[...], preferred_element_type=F32)
+        sums = wide[0:ROWS] + (wide[ROWS:] + thin)
+        for i in range(WIDE):
+            part[b, WIDE * h + i] = sums[:, i * LANES : (i + 1) * LANES]
+        pair_swap(b, h).start()
 
     @pl.loop(0, NB + DEPTH)
     def _(t):
-        for h in range(2):
+        for h in range(NH):
 
             def only(late, act):
-                b, part_of = t + (h - late) // 2, (h - late) % 2
+                b, part_of = t + (h - late) // NH, (h - late) % NH
 
                 @pl.when(jnp.logical_and(b >= 0, b < NB))
                 def _():
@@ -460,10 +457,8 @@
             only(LATE[2], onward(1))
             only(LATE[3], onward(0))
             only(0, expand)
-            only(0, multiply(0))
+            only(0, multiply)
             only(1, begin)
-            if len(DOTS[h]) > 1:
-                only(0, multiply(1))
 
     for d in range(1, PAIRS):
         source = lax.rem(p + d, PAIRS)
@@ -478,13 +473,14 @@
 
     @pl.loop(0, NB)
     def _(b):
-        for h in range(2):
+        for h in range(NH):
             pair_swap(b, h).wait_send()
             for k in range(STEPS_A):
                 chain_a(b, h, k).wait_send()
             for k in range(STEPS_B):
                 chain_b(b, h, k).wait_send()
-            there, copy = outward(b, h)
+        for g in range(len(FIRST)):
+            there, copy = outward(b, g)
 
             @pl.when(there != p)
             def _():
@@ -492,7 +488,7 @@
 
             @pl.when(there == p)
             def _():
-                homeward(b, h).wait()
+                homeward(b, g).wait()
 
     for copy in sends:
         copy.wait_send()
@@ -554,8 +550,8 @@
             pltpu.VMEM((KC // 2, ROWS, LANES), F32),
             pltpu.VMEM((2 * ROWS, KDIM), BF16),
             pltpu.VMEM((PAIRS + 1, 4, SHARD, LANES), BF16),
-            pltpu.VMEM((KDIM, PL * LANES), BF16),
-            pltpu.VMEM((KDIM, PL * LANES), BF16),
+            pltpu.VMEM((KDIM, WIDE * LANES), BF16),
+            pltpu.VMEM((KDIM, WIDE * LANES), BF16),
             pltpu.VMEM((NB, PL, ROWS, LANES), F32),
             pltpu.VMEM((NB, PL, HALF, LANES), F32),
             pltpu.VMEM((NB, STEPS_A, PL, CH, LANES), F32),
@@ -567,13 +563,13 @@
             dma,
             dma((PAIRS,)),
             dma((PAIRS,)),
-            dma((NB, len(PARTS))),
-            dma((NB, len(PARTS))),
-            dma((NB, 2, STEPS_A)),
-            dma((NB, 2, STEPS_A)),
-            dma((NB, 2, STEPS_B)),
-            dma((NB, 2, STEPS_B)),
-            dma((NB, 2)),
+            dma((NB, NH)),
+            dma((NB, NH)),
+            dma((NB, NH, STEPS_A)),
+            dma((NB, NH, STEPS_A)),
+            dma((NB, NH, STEPS_B)),
+            dma((NB, NH, STEPS_B)),
+            dma((NB, len(FIRST))),
             dma((PAIRS,)),
             dma,
         ],

time: 128 us -> 123 us (0.961)
  Pallas kernels: 128 us -> 123 us
    pallas_call x1, Pallas kernels: 125 us -> 120 us  [on_device(): pl.pallas_call(main_kernel, out_shape=jax.ShapeDtypeStruct((3, PAIRS * CH...]
where the time goes in v2:
time: 123 us
  Pallas kernels  123 us (100%)
    pallas_call x1, Pallas kernels, on_device(): pl.pallas_call(main_kernel, out_shape=jax.ShapeDtypeStruct((3, PAIRS * CH...  120 us
    pallas_call x1, Pallas kernels, on_device(): pl.pallas_call(pick_kernel, out_shape=jax.ShapeDtypeStruct((CW, PAIRS * R...  2.6 us

profile of v2, /device:TPU:8, one launch (start us, length us, event | category | flops | bytes accessed | tf_op | source)
XLA Modules:
  0.0 122.8 jit_solution(17658970735144152547)
XLA Ops:
  0.0 120.2 %cycle.1.rows_ref = f32[3,640,128]{2,1,0:T(8,128)} custom-call(f32[640,128]{1,0:T(8,128)} %bitcast.6, s32[1,20]{1,0:T(1,128)} %bitcast.8, f32[5,8,8192]{2,1,0:T(8,128)} %w_ref.1, s32[5,8]{1,0:T(8,128)} %w_cols_ref.1), custom_call_target="tpu_custom_call" | custom-call | tf_op jit(solution)/shard_map/cycle/pallas_call | solution.py:537
  120.2 2.6 %pick.1 = f32[5,80,512]{2,1,0:T(8,128)} custom-call(f32[3,640,128]{2,1,0:T(8,128)} %cycle.1.rows_ref, s32[5,1,80]{2,1,0:T(1,128)} %bitcast.7), custom_call_target="tpu_custom_call" | custom-call | tf_op jit(solution)/shard_map/pick/pallas_call | solution.py:581

commit v3 on v2

--- a/solution.py
+++ b/solution.py
@@ -244,9 +244,9 @@
     def halve(half, da, db):
         place = slot(half, da, db)
 
-        @pl.loop(half * 4, half * 4 + 4, unroll=4)
+        @pl.loop(half * 2, half * 2 + 2, unroll=2)
         def _(n):
-            rows = pl.ds(pl.multiple_of(n * 80, 80), 80)
+            rows = pl.ds(pl.multiple_of(n * 160, 160), 160)
             x = tiles[place, rows, :]
             for h, wide in enumerate((x, pltpu.roll(x, S, 1))):
                 high, low = split(wide)
@@ -295,14 +295,6 @@
         for sign in both:
             for half in range(2):
                 halve(half, da, -sign)
-    halves[PAIRS] = jnp.zeros((4, SHARD, LANES), BF16)
-    for w in range(KC // 2):
-        w_split(w)
-    for sign in both:
-        for half in range(2):
-            got(half, "b0", 2, sign)
-            go(half, "b1", 2, sign)
-
     for d in range(1, PAIRS):
         get_ids(d).wait_recv()
     tile_at = lax.broadcasted_iota(jnp.int32, (COLS, LANES), 0)
@@ -312,7 +304,15 @@
     inv_vec[...] = found
     table = pltpu.make_async_copy(inv_vec, inv, inv_sem)
     table.start()
+    halves[PAIRS] = jnp.zeros((4, SHARD, LANES), BF16)
+    for w in range(KC // 2):
+        w_split(w)
     table.wait()
+    for sign in both:
+        for half in range(2):
+            got(half, "b0", 2, sign)
+            go(half, "b1", 2, sign)
+
     for sign in both:
         for half in range(2):
             halve(half, 2, -sign)

time: 123 us -> 123 us (level)
  no operation moved by 1% of the time
where the time goes in v3:
time: 123 us
  Pallas kernels  123 us (100%)
    pallas_call x1, Pallas kernels, on_device(): pl.pallas_call(main_kernel, out_shape=jax.ShapeDtypeStruct((3, PAIRS * CH...  120 us
    pallas_call x1, Pallas kernels, on_device(): pl.pallas_call(pick_kernel, out_shape=jax.ShapeDtypeStruct((CW, PAIRS * R...  2.6 us

profile of v3, /device:TPU:8, one launch (start us, length us, event | category | flops | bytes accessed | tf_op | source)
XLA Modules:
  0.0 122.8 jit_solution(4298395798507478539)
XLA Ops:
  0.0 120.2 %cycle.1.rows_ref = f32[3,640,128]{2,1,0:T(8,128)} custom-call(f32[640,128]{1,0:T(8,128)} %bitcast.6, s32[1,20]{1,0:T(1,128)} %bitcast.8, f32[5,8,8192]{2,1,0:T(8,128)} %w_ref.1, s32[5,8]{1,0:T(8,128)} %w_cols_ref.1), custom_call_target="tpu_custom_call" | custom-call | tf_op jit(solution)/shard_map/cycle/pallas_call | solution.py:537
  120.2 2.6 %pick.1 = f32[5,80,512]{2,1,0:T(8,128)} custom-call(f32[3,640,128]{2,1,0:T(8,128)} %cycle.1.rows_ref, s32[5,1,80]{2,1,0:T(1,128)} %bitcast.7), custom_call_target="tpu_custom_call" | custom-call | tf_op jit(solution)/shard_map/pick/pallas_call | solution.py:581
